TPU v7x, 256 devices: a whole 4x4x8 slice. The times are simulated.
256 devices in a mesh: sector: 16 (over x, y_lo, core), block: 16 (over z, y_hi).
Axes of the slice: x: 4, y: 4 (y_hi: 2, y_lo: 2; y = y_hi * 2 + y_lo), z: 8, core: 2. Of those that a mesh axis runs over, the one named last changes fastest.
Arguments:
- flow: float32 [5, 4, 256, 2048], P(None, None, 'block', 'sector'), may hold values from -1 to 5, as said below
- adjoint: float32 [5, 4, 256, 2048], P(None, None, 'block', 'sector'), may hold values from -6 to 6
- adjoint_later: float32 [2, 5, 4, 256, 2048], P(None, None, None, 'block', 'sector'), may hold values from -6 to 6
- objective_grad: float32 [5, 4, 256, 2048], P(None, None, 'block', 'sector'), may hold values from -12 to 12
- volume: float32 [4, 256, 2048], P(None, 'block', 'sector'), may hold values from 0.5 to 2
- panel_maps: float32 [4, 4, 128, 128], replicated, may hold values from 0 to 1, as said below
- rotor_step: int32 [1], replicated, may hold values from 0 to 63
Outputs:
- updated_adjoint: float32 [5, 4, 256, 2048], P(None, None, 'block', 'sector')
Inputs may be any that keep to these rules, and one draw needn't show every extreme that they name: `flow`: density and pressure are positive in every cell. `panel_maps`: entries are non-negative.
All inputs are finite; a program needn't handle non-finite values.
Results may differ from a plain program's by a relative error of at most 0.000057.
Values sent between devices are 32-bit elements; how exact they have to be, the bound alone decides.
A program may use at most 64 MiB of HBM per device.

v0:
```python
from functools import partial

import jax
import jax.numpy as jnp
from jax import lax
from jax.sharding import PartitionSpec as P

PHASES = 4
ITERS = 4


gamma_gas = 1.4
second_coef = 0.5
fourth_coef = 1.0 / 32.0
courant = 0.6
physical_step = 2.0
sensor_floor = 0.0001
highest = lax.Precision.HIGHEST


def passed_along(x, axis, by):
    length = lax.axis_size(axis)
    return lax.ppermute(x, axis, [(i, (i + by) % length) for i in range(length)])


def with_halo(block, sides, width):
    for axis, dim in sides:
        count = lax.axis_size(axis)
        forward = [(i, i + 1) for i in range(count - 1)]
        forward.append((count - 1, 0))
        backward = [(target, source) for source, target in forward]
        low = lax.ppermute(
            lax.slice_in_dim(block, block.shape[dim] - width, None, axis=dim), axis, forward
        )
        high = lax.ppermute(lax.slice_in_dim(block, 0, width, axis=dim), axis, backward)
        block = jnp.concatenate([low, block, high], axis=dim)
    return block


def pressure(state):
    density = state[0]
    kinetic = 0.5 * (state[1] * state[1] + state[2] * state[2] + state[3] * state[3]) / density
    return (gamma_gas - 1.0) * (state[4] - kinetic)


def slab(array, start, stop, axis):
    return lax.slice_in_dim(array, start, stop, axis=axis)


def direction_terms(wide, axis, momentum_row):
    density = wide[0]
    pressure_now = pressure(wide)
    speed = wide[momentum_row] / density
    sound_speed = jnp.sqrt(gamma_gas * pressure_now / density)
    radius = jnp.sqrt(speed * speed + 0.01) + sound_speed
    fluxes = [
        wide[momentum_row],
        wide[1] * speed,
        wide[2] * speed,
        wide[3] * speed,
        (wide[4] + pressure_now) * speed,
    ]
    fluxes[momentum_row] = fluxes[momentum_row] + pressure_now
    flux = jnp.stack(fluxes)
    scalar_axis = axis - 1
    length = pressure_now.shape[scalar_axis]
    upper_p = slab(pressure_now, 2, length, scalar_axis)
    middle_p = slab(pressure_now, 1, length - 1, scalar_axis)
    lower_p = slab(pressure_now, 0, length - 2, scalar_axis)
    bend = upper_p - 2.0 * middle_p + lower_p
    total = upper_p + 2.0 * middle_p + lower_p
    sensor = jnp.sqrt(bend * bend + sensor_floor) / total
    second_damp = (
        second_coef
        * 0.5
        * (slab(sensor, 0, length - 3, scalar_axis) + slab(sensor, 1, length - 2, scalar_axis))
    )
    fourth_damp = fourth_coef * fourth_coef / (fourth_coef + second_damp)
    spectral = 0.5 * (
        slab(radius, 1, length - 2, scalar_axis) + slab(radius, 2, length - 1, scalar_axis)
    )
    behind = slab(wide, 0, length - 3, axis)
    left_cell = slab(wide, 1, length - 2, axis)
    right_cell = slab(wide, 2, length - 1, axis)
    ahead = slab(wide, 3, length, axis)
    damping = spectral * (
        second_damp * (right_cell - left_cell)
        - fourth_damp * (ahead - 3.0 * right_cell + 3.0 * left_cell - behind)
    )
    face = 0.5 * (slab(flux, 1, length - 2, axis) + slab(flux, 2, length - 1, axis)) - damping
    faces = length - 3
    change = slab(face, 1, faces, axis) - slab(face, 0, faces - 1, axis)
    return (change, slab(radius, 2, length - 2, scalar_axis))


def residual_and_radius(padded):
    full = jnp.pad(padded, ((0, 0), (2, 2), (0, 0), (0, 0)), mode="edge")
    axial_change, axial_radius = direction_terms(full[:, 2:-2, :, 2:-2], 2, 1)
    turning_change, turning_radius = direction_terms(full[:, 2:-2, 2:-2, :], 3, 2)
    radial_change, radial_radius = direction_terms(full[:, :, 2:-2, 2:-2], 1, 3)
    return (
        axial_change + turning_change + radial_change,
        axial_radius + turning_radius + radial_radius,
    )


def apply_pair(nearer, farther, first_map, second_map):
    return jnp.einsum("...i,ti->...t", nearer, first_map, precision=highest) + jnp.einsum(
        "...i,ti->...t", farther, second_map, precision=highest
    )


def apply_pair_back(nearer, farther, first_map, second_map):
    return jnp.einsum("...t,ti->...i", nearer, first_map, precision=highest) + jnp.einsum(
        "...t,ti->...i", farther, second_map, precision=highest
    )


def partners(down_piece, up_piece, offset):
    count = lax.axis_size("sector")
    near_turn = offset % count
    far_turn = (offset + 1) % count

    def advance(step, carry):
        down_now, up_now, down_near, down_far, up_near, up_far = carry
        down_now = passed_along(down_now, "sector", 1)
        up_now = passed_along(up_now, "sector", -1)
        travelled = (step + 1) % count
        down_near = jnp.where(travelled == near_turn, down_now, down_near)
        down_far = jnp.where(travelled == far_turn, down_now, down_far)
        up_near = jnp.where(travelled == near_turn, up_now, up_near)
        up_far = jnp.where(travelled == far_turn, up_now, up_far)
        return (down_now, up_now, down_near, down_far, up_near, up_far)

    empty_down = jnp.zeros_like(down_piece)
    empty_up = jnp.zeros_like(up_piece)
    start = (down_piece, up_piece, empty_down, empty_down, empty_up, empty_up)
    result = lax.fori_loop(0, count, advance, start)
    return (result[2], result[3], result[4], result[5])


def local_residual(
    state, lower_raw, upper_raw, left_side, right_side, lower_face, upper_face, flags
):
    at_inlet, at_outlet, stator_face, rotor_face = flags
    lower = jnp.where(
        at_inlet,
        jnp.repeat(state[:, :, :1], 2, axis=2),
        jnp.where(stator_face, lower_face, lower_raw),
    )
    upper = jnp.where(
        at_outlet,
        jnp.repeat(state[:, :, -1:], 2, axis=2),
        jnp.where(rotor_face, upper_face, upper_raw),
    )
    column = jnp.concatenate([lower, state, upper], axis=2)
    margin = ((0, 0), (0, 0), (2, 2), (0, 0))
    padded = jnp.concatenate(
        [jnp.pad(left_side, margin), column, jnp.pad(right_side, margin)], axis=3
    )
    return residual_and_radius(padded)


def shards(flow, adjoint, adjoint_later, objective_grad, volume, panel_maps, rotor_step):
    blocks = lax.axis_size("block")
    place = lax.axis_index("block")
    turn = rotor_step[0]
    offset = turn // PHASES
    maps = lax.dynamic_index_in_dim(panel_maps, turn % PHASES, 0, keepdims=False)
    half = blocks // 2
    flags = (place == 0, place == blocks - 1, place == half, place == half - 1)
    padded = with_halo(flow, (("sector", 3), ("block", 2)), 2)
    lower_raw = padded[:, :, :2, 2:-2]
    upper_raw = padded[:, :, -2:, 2:-2]
    left_side = padded[:, :, 2:-2, :2]
    right_side = padded[:, :, 2:-2, -2:]
    down_near, down_far, up_near, up_far = partners(lower_raw, upper_raw, offset)
    lower_face = apply_pair(down_near, down_far, maps[0], maps[1])
    upper_face = apply_pair(up_near, up_far, maps[2], maps[3])
    local = partial(local_residual, flags=flags)
    change, pullback, radius_sum = jax.vjp(
        local,
        flow,
        lower_raw,
        upper_raw,
        left_side,
        right_side,
        lower_face,
        upper_face,
        has_aux=True,
    )
    factor = courant / (radius_sum + 1.5 * courant * volume / physical_step)
    source = (
        objective_grad + volume * (2.0 * adjoint_later[0] - 0.5 * adjoint_later[1]) / physical_step
    )
    margin = ((0, 0), (0, 0), (2, 2), (0, 0))
    current = adjoint
    for sweep in range(ITERS):
        (
            own_terms,
            back_lower,
            back_upper,
            back_left,
            back_right,
            back_lower_face,
            back_upper_face,
        ) = pullback(current)
        high_near, high_far, low_near, low_far = partners(back_upper_face, back_lower_face, offset)
        lower_send = back_lower + apply_pair_back(low_near, low_far, maps[0], maps[1])
        upper_send = back_upper + apply_pair_back(high_near, high_far, maps[2], maps[3])
        column = jnp.concatenate([lower_send, own_terms, upper_send], axis=2)
        sheet = jnp.concatenate(
            [jnp.pad(back_left, margin), column, jnp.pad(back_right, margin)], axis=3
        )
        arrived = with_halo(sheet, (("sector", 3), ("block", 2)), 2)
        transposed = own_terms
        transposed = transposed.at[:, :, :2].add(arrived[:, :, 0:2, 4:-4])
        transposed = transposed.at[:, :, -2:].add(arrived[:, :, -2:, 4:-4])
        transposed = transposed.at[:, :, :, :2].add(arrived[:, :, 4:-4, 0:2])
        transposed = transposed.at[:, :, :, -2:].add(arrived[:, :, 4:-4, -2:])
        current = current - factor * (1.5 * volume * current / physical_step + transposed - source)
    return current


def solution(mesh):
    placed = (
        P(None, None, "block", "sector"),
        P(None, None, "block", "sector"),
        P(None, None, None, "block", "sector"),
        P(None, None, "block", "sector"),
        P(None, "block", "sector"),
        P(),
        P(),
    )
    return jax.shard_map(
        shards,
        mesh=mesh,
        in_specs=placed,
        out_specs=P(None, None, "block", "sector"),
        check_vma=False,
    )
```

profile of v0, /device:TPU:64, one launch (start us, length us, event | category | flops | bytes accessed | tf_op | source)
XLA Modules:
  0.0 732.1 jit_solution(1347312187007294941)
XLA Ops:
  7.4 4.0 collective-permute-done.10
  20.1 89.5 %while.146 = (s32[]{:T(128)}, f32[5,4,2,128]{3,2,1,0:T(2,128)S(1)}, f32[5,4,2,128]{3,2,1,0:T(2,128)S(1)}, f32[5,4,2,128]{3,2,1,0:T(2,128)S(1)}, f32[5,4,2,128]{3...) while((s32[]{:T(128)}, f32[5,4,2,128]{3,2,1,0:T(2,128)S(1)}, ...), condition=%wide.region_1.2_spmd.clone, body=%wide.region_0.1_spmd.clone.sunk | while | flops 40976 | bytes 450915 | solution.py:138
  25.7 3.9 collective-permute-start.1
  31.3 3.9 collective-permute-start.1
  36.9 3.9 collective-permute-start.1
  64.8 3.9 collective-permute-start.1
  70.3 3.9 collective-permute-start.1
  75.9 3.9 collective-permute-start.1
  81.5 3.9 collective-permute-start.1
  87.1 3.9 collective-permute-start.1
  132.2 100.2 %while.147 = (s32[]{:T(128)}, f32[5,4,2,128]{3,2,1,0:T(2,128)S(1)}, f32[5,4,2,128]{3,2,1,0:T(2,128)S(1)}, f32[5,4,2,128]{3,2,1,0:T(2,128)S(1)}, f32[5,4,2,128]{3...) while((s32[]{:T(128)}, f32[5,4,2,128]{3,2,1,0:T(2,128)S(1)}, ...), condition=%wide.region_16.18_spmd.clone, body=%wide.region_15.17_spmd.clone.sunk | while | flops 40976 | bytes 450915 | solution.py:138
  143.4 3.9 collective-permute-start.3
  149.0 3.9 collective-permute-start.3
  160.1 3.9 collective-permute-start.3
  171.2 3.9 collective-permute-start.3
  182.4 3.9 collective-permute-start.3
  188.0 3.9 collective-permute-start.3
  199.1 3.9 collective-permute-start.3
  210.3 3.9 collective-permute-start.3
  215.8 3.9 collective-permute-start.3
  227.0 3.9 collective-permute-start.3
  254.7 4.1 scatter-add.56
  259.8 14.4 %scatter-add.59 = f32[5,4,16,128]{3,1,2,0:T(4,128)S(1)} dynamic-update-slice(f32[5,4,16,128]{3,1,2,0:T(4,128)S(1)} %scatter-add.56, f32[5,4,16,2]{3,1,2,0:T(4,128)S(1)} %slice_add_fusion.13, s32[]{:T(128)} %constant.707.clone.1, s32[]{:T(128)} %constant.707.clone.1, s32[]{:T(128)} %constant.707.clone.1, s32[]{:T(128)} %constant.733.clone.1) | dynamic-update-slice | bytes 5124 | tf_op jit(solution)/shard_map/scatter-add | solution.py:220
  297.0 90.0 %while.148 = (s32[]{:T(128)}, f32[5,4,2,128]{3,2,1,0:T(2,128)S(1)}, f32[5,4,2,128]{3,2,1,0:T(2,128)S(1)}, f32[5,4,2,128]{3,2,1,0:T(2,128)S(1)}, f32[5,4,2,128]{3...) while((s32[]{:T(128)}, f32[5,4,2,128]{3,2,1,0:T(2,128)S(1)}, ...), condition=%wide.region_29.31_spmd.clone, body=%wide.region_28.30_spmd.clone.sunk | while | flops 40976 | bytes 450915 | solution.py:138
  297.5 3.9 collective-permute-start.5
  309.1 3.9 collective-permute-start.5
  314.7 3.9 collective-permute-start.5
  325.8 3.9 collective-permute-start.5
  336.9 3.9 collective-permute-start.5
  348.1 3.9 collective-permute-start.5
  353.7 3.9 collective-permute-start.5
  364.8 3.9 collective-permute-start.5
  376.0 3.9 collective-permute-start.5
  381.5 3.9 collective-permute-start.5
  387.4 3.9 collective-permute-start.19
  408.8 4.1 scatter-add.64
  414.0 14.4 %scatter-add.65 = f32[5,4,16,128]{3,1,2,0:T(4,128)S(1)} dynamic-update-slice(f32[5,4,16,128]{3,1,2,0:T(4,128)S(1)} %scatter-add.64, f32[5,4,16,2]{3,1,2,0:T(4,128)S(1)} %slice_add_fusion.10, s32[]{:T(128)} %constant.707.clone.1, s32[]{:T(128)} %constant.707.clone.1, s32[]{:T(128)} %constant.707.clone.1, s32[]{:T(128)} %constant.733.clone.1) | dynamic-update-slice | bytes 5124 | tf_op jit(solution)/shard_map/scatter-add | solution.py:220
  451.0 89.9 %while.149 = (s32[]{:T(128)}, f32[5,4,2,128]{3,2,1,0:T(2,128)S(1)}, f32[5,4,2,128]{3,2,1,0:T(2,128)S(1)}, f32[5,4,2,128]{3,2,1,0:T(2,128)S(1)}, f32[5,4,2,128]{3...) while((s32[]{:T(128)}, f32[5,4,2,128]{3,2,1,0:T(2,128)S(1)}, ...), condition=%wide.region_42.44_spmd.clone, body=%wide.region_41.43_spmd.clone.sunk | while | flops 40976 | bytes 450915 | solution.py:138
  451.2 3.9 collective-permute-start.7
  463.0 3.9 collective-permute-start.7
  474.2 3.9 collective-permute-start.7
  485.3 3.9 collective-permute-start.7
  552.9 4.4 collective-permute-start.24
  563.9 4.1 scatter-add.70
  569.1 14.4 %scatter-add.71 = f32[5,4,16,128]{3,1,2,0:T(4,128)S(1)} dynamic-update-slice(f32[5,4,16,128]{3,1,2,0:T(4,128)S(1)} %scatter-add.70, f32[5,4,16,2]{3,1,2,0:T(4,128)S(1)} %slice_add_fusion.7, s32[]{:T(128)} %constant.707.clone.1, s32[]{:T(128)} %constant.707.clone.1, s32[]{:T(128)} %constant.707.clone.1, s32[]{:T(128)} %constant.733.clone.1) | dynamic-update-slice | bytes 5124 | tf_op jit(solution)/shard_map/scatter-add | solution.py:220
  604.8 90.4 %while.150 = (s32[]{:T(128)}, f32[5,4,2,128]{3,2,1,0:T(2,128)S(1)}, f32[5,4,2,128]{3,2,1,0:T(2,128)S(1)}, f32[5,4,2,128]{3,2,1,0:T(2,128)S(1)}, f32[5,4,2,128]{3...) while((s32[]{:T(128)}, f32[5,4,2,128]{3,2,1,0:T(2,128)S(1)}, ...), condition=%wide.region_55.57_spmd.clone, body=%wide.region_54.56_spmd.clone.sunk | while | flops 40976 | bytes 450915 | solution.py:138
  712.4 4.1 scatter-add.76
  716.6 14.4 %scatter-add.79 = f32[5,4,16,128]{3,1,2,0:T(4,128)S(1)} dynamic-update-slice(f32[5,4,16,128]{3,1,2,0:T(4,128)S(1)} %scatter-add.76, f32[5,4,16,2]{3,1,2,0:T(4,128)S(1)} %slice_add_fusion.4, s32[]{:T(128)} %constant.707.clone.1, s32[]{:T(128)} %constant.707.clone.1, s32[]{:T(128)} %constant.707.clone.1, s32[]{:T(128)} %constant.733.clone.1) | dynamic-update-slice | bytes 5124 | tf_op jit(solution)/shard_map/scatter-add | solution.py:220
  (1243 shorter events, 502.8 us)
Async XLA Ops:
  1.3 6.1 collective-permute-start.11
  4.5 6.9 collective-permute-start.10
  11.5 6.5 collective-permute-start.12
  14.5 5.5 collective-permute-start.13
  25.7 5.4 collective-permute-start.1
  31.3 5.4 collective-permute-start.1
  36.9 5.4 collective-permute-start.1
  42.5 5.4 collective-permute-start.1
  48.0 5.4 collective-permute-start.1
  53.6 5.4 collective-permute-start.1
  59.2 5.4 collective-permute-start.1
  64.8 5.4 collective-permute-start.1
  70.3 5.4 collective-permute-start.1
  87.1 5.4 collective-permute-start.1
  130.7 110.4 %collective-permute-start.14 = (f32[5,4,20,2]{3,1,2,0:T(4,128)}, f32[5,4,20,2]{3,1,2,0:T(4,128)}, u32[]{:S(2)}, u32[]{:S(2)}) collective-permute-start(f32[5,4,20,2]{3,1,2,0:T(4,128)} %pad.1270), channel_id=1, source_target_pairs={{0,16},{16,32},{32,48},{48,64},{64,80},{80,96},{96,112},{112,128},... | collective-permute-start | bytes 9608 | tf_op jit(solution)/shard_map/ppermute | solution.py:32
  143.3 5.4 collective-permute-start.2
  143.4 5.4 collective-permute-start.3
  182.4 5.4 collective-permute-start.3
  210.3 5.4 collective-permute-start.3
  233.4 7.7 %collective-permute-start.15 = (f32[5,4,20,2]{3,1,2,0:T(4,128)S(1)}, f32[5,4,20,2]{3,1,2,0:T(4,128)}, u32[]{:S(2)}, u32[]{:S(2)}) collective-permute-start(f32[5,4,20,2]{3,1,2,0:T(4,128)S(1)} %copy-done.133), channel_id=1, source_target_pairs={{16,0},{32,16},{48,32},{64,48},{80,64},{96,80},{112,96},{128,112},... | collective-permute-start | bytes 9608 | tf_op jit(solution)/shard_map/ppermute | solution.py:35
  244.4 6.4 collective-permute-start.16
  248.1 5.5 collective-permute-start.17
  295.6 99.6 %collective-permute-start.18 = (f32[5,4,20,2]{3,1,2,0:T(4,128)}, f32[5,4,20,2]{3,1,2,0:T(4,128)}, u32[]{:S(2)}, u32[]{:S(2)}) collective-permute-start(f32[5,4,20,2]{3,1,2,0:T(4,128)} %pad.1360), channel_id=1, source_target_pairs={{0,16},{16,32},{32,48},{48,64},{64,80},{80,96},{96,112},{112,128},... | collective-permute-start | bytes 9608 | tf_op jit(solution)/shard_map/ppermute | solution.py:32
  297.4 6.0 collective-permute-start.4
  297.5 5.9 collective-permute-start.5
  309.1 5.4 collective-permute-start.5
  348.1 5.4 collective-permute-start.5
  376.0 5.4 collective-permute-start.5
  387.4 7.8 %collective-permute-start.19 = (f32[5,4,20,2]{3,1,2,0:T(4,128)}, f32[5,4,20,2]{3,1,2,0:T(4,128)}, u32[]{:S(2)}, u32[]{:S(2)}) collective-permute-start(f32[5,4,20,2]{3,1,2,0:T(4,128)} %pad.1362), channel_id=1, source_target_pairs={{16,0},{32,16},{48,32},{64,48},{80,64},{96,80},{112,96},{128,112},... | collective-permute-start | bytes 9608 | tf_op jit(solution)/shard_map/ppermute | solution.py:35
  398.5 6.4 collective-permute-start.20
  402.2 5.5 collective-permute-start.21
  449.5 100.1 %collective-permute-start.22 = (f32[5,4,20,2]{3,1,2,0:T(4,128)}, f32[5,4,20,2]{3,1,2,0:T(4,128)}, u32[]{:S(2)}, u32[]{:S(2)}) collective-permute-start(f32[5,4,20,2]{3,1,2,0:T(4,128)} %pad.1450), channel_id=1, source_target_pairs={{0,16},{16,32},{32,48},{48,64},{64,80},{80,96},{96,112},{112,128},... | collective-permute-start | bytes 9608 | tf_op jit(solution)/shard_map/ppermute | solution.py:32
  451.1 6.2 collective-permute-start.6
  451.2 6.1 collective-permute-start.7
  485.3 5.4 collective-permute-start.7
  524.3 5.4 collective-permute-start.7
  541.9 7.7 %collective-permute-start.23 = (f32[5,4,20,2]{3,1,2,0:T(4,128)S(1)}, f32[5,4,20,2]{3,1,2,0:T(4,128)}, u32[]{:S(2)}, u32[]{:S(2)}) collective-permute-start(f32[5,4,20,2]{3,1,2,0:T(4,128)S(1)} %copy-done.134), channel_id=1, source_target_pairs={{16,0},{32,16},{48,32},{64,48},{80,64},{96,80},{112,96},{128,112},... | collective-permute-start | bytes 9608 | tf_op jit(solution)/shard_map/ppermute | solution.py:35
  552.9 6.4 collective-permute-start.24
  557.3 5.5 collective-permute-start.25
  603.9 96.3 %collective-permute-start.26 = (f32[5,4,20,2]{3,1,2,0:T(4,128)S(1)}, f32[5,4,20,2]{3,1,2,0:T(4,128)S(1)}, u32[]{:S(2)}, u32[]{:S(2)}) collective-permute-start(f32[5,4,20,2]{3,1,2,0:T(4,128)S(1)} %pad.1540), channel_id=1, source_target_pairs={{0,16},{16,32},{32,48},{48,64},{64,80},{80,96},{96,112},{112,128},... | collective-permute-start | bytes 9608 | tf_op jit(solution)/shard_map/ppermute | solution.py:32
  605.0 6.6 collective-permute-start.8
  605.1 6.5 collective-permute-start.9
  628.4 5.4 collective-permute-start.9
  667.4 5.4 collective-permute-start.9
  689.6 5.4 collective-permute-start.8
  695.6 7.2 collective-permute-start.27
  703.7 6.5 collective-permute-start.28
  706.7 5.5 collective-permute-start.29
  (292 other events, 1887.2 us)
where the time goes:
time: 740 us; the launch traced here: 732 us
  starting transfers between devices  361 us (49%)
  waiting for transfers between devices  148 us (20%)
  local copies, waits for them, and re-layouts  140 us (19%)
  other arithmetic  56.4 us (8%)
  loops' own time  14.3 us (2%)
  matrix products  9.05 us (1%)
    ppermute x160, starting transfers between devices, passed_along(): lax.ppermute(x, axis, [(i, (i + by) % length) for i in range(length)])  319 us
    ppermute x160, waiting for transfers between devices, passed_along(): lax.ppermute(x, axis, [(i, (i + by) % length) for i in range(length)])  121 us
    scatter-add x4, local copies, waits for them, and re-layouts, shards(): transposed = transposed.at[:, :, :, -2:].add(arrived[:, :, 4:-4, -2:])  57.8 us
    unnamed x332, local copies, waits for them, and re-layouts  45.4 us
    ppermute x10, starting transfers between devices, with_halo(): lax.ppermute(lax.slice_in_dim(block, 0, width, axis=dim), axis, backward)  24.1 us
    ppermute x10, starting transfers between devices, with_halo(): lax.ppermute(lax.slice_in_dim(block, block.shape[dim] - width, None, axis...  17.1 us
    ppermute x10, waiting for transfers between devices, with_halo(): lax.ppermute(lax.slice_in_dim(block, 0, width, axis=dim), axis, backward)  16.3 us
    scatter-add x4, local copies, waits for them, and re-layouts, shards(): transposed = transposed.at[:, :, :, :2].add(arrived[:, :, 4:-4, 0:2])  16.2 us
  transfers between devices with their start and end apart: 180, of which 166 were waited for; matrix products, arithmetic and copies ran while one was open for 3% of the time, Pallas kernels for 0%

commit v1 on v0

v1 whole, which is shorter than its diff:
```python
import functools

import jax
import jax.numpy as jnp
from jax import lax
from jax.experimental import pallas as pl
from jax.experimental.pallas import tpu as pltpu
from jax.sharding import PartitionSpec as P

PHASES = 4
ITERS = 4
ROUNDS = ITERS + 1
CHOICES = 16

FOURTH = 1.0 / 32.0
MESH = pl.DeviceIdType.MESH
HIGHEST = lax.Precision.HIGHEST

RINV, V1, V2, V3, ENTH, RP, RR, KE, NCELL = 0, 1, 2, 3, 4, 5, 6, 7, 8
LE2, LE4, DD, EE, N1, N0, RQ, NDIR = 0, 1, 2, 7, 12, 13, 14, 15


def cell_terms(u):
    rinv = 1.0 / u[0]
    v = [u[m] * rinv for m in (1, 2, 3)]
    ke = 0.5 * (v[0] * v[0] + v[1] * v[1] + v[2] * v[2])
    p = 0.4 * (u[4] - ke * u[0])
    c = jnp.sqrt(1.4 * p * rinv)
    return rinv, v, ke, p, c, 0.7 * rinv / c, -0.5 * c * rinv


def sensor_terms(below, here, above):
    bend = above - 2.0 * here + below
    tinv = 1.0 / (above + 2.0 * here + below)
    root = jnp.sqrt(bend * bend + 1e-4)
    nu = root * tinv
    by_bend = bend * tinv / root
    by_total = -nu * tinv
    return nu, 0.25 * (by_bend + by_total), 0.5 * (by_total - by_bend)


def face_terms(nu_low, nu_high, rad_low, rad_high, d1, d3):
    e2 = 0.25 * (nu_low + nu_high)
    e4 = FOURTH * FOURTH / (FOURTH + e2)
    lam = 0.5 * (rad_low + rad_high)
    slope = e4 * e4 * (1.0 / (FOURTH * FOURTH))
    dd = [-0.5 * (e2 * a - e4 * b) for a, b in zip(d1, d3)]
    ee = [-lam * (a + slope * b) for a, b in zip(d1, d3)]
    return [lam * e2, lam * e4] + dd + ee


def shifts(axis, length):
    def up(v):
        return pltpu.roll(v, length - 1, axis)

    def down(v):
        return pltpu.roll(v, 1, axis)

    return up, down


def direction_coefs(u, p, c, q, up, down):
    sq = jnp.sqrt(q * q + 0.01)
    radius = sq + c
    nu, n1, n0 = sensor_terms(down(p), p, up(p))
    d1 = [up(a) - a for a in u]
    d3 = [up(a) - 2.0 * a + down(a) for a in d1]
    faces = face_terms(nu, up(nu), radius, up(radius), d1, d3)
    return faces + [n1, n0, q / sq], radius


def dot5(a, b):
    return (a[0] * b[0] + a[1] * b[1]) + (a[2] * b[2] + a[3] * b[3]) + a[4] * b[4]


def direction_apply(lam, cf, cell, u, m, up, down):
    w = [a - up(a) for a in lam]
    lb = dot5(w, [cf(DD + v) for v in range(5)])
    eb = dot5(w, [cf(EE + v) for v in range(5)])
    rb = lb + down(lb)
    nub = eb + down(eb)
    t1 = nub * cf(N1)
    phi = [0.5 * (a + down(a)) for a in w]
    q = cell(V1 + m - 1)
    qb = rb * cf(RQ) + phi[1] * u(1) + phi[2] * u(2) + phi[3] * u(3) + phi[4] * cell(ENTH)
    pb = up(t1) + down(t1) + nub * cf(N0) + rb * cell(RP) + phi[4] * q + phi[m]
    le2, le4 = cf(LE2), cf(LE4)
    out = []
    for v in range(5):
        far = le4 * w[v]
        z = up(far) + down(far) - 2.0 * far - le2 * w[v]
        out.append(down(z) - z)
    qr = qb * cell(RINV)
    out[0] = out[0] + rb * cell(RR) - qr * q
    for v in range(1, 5):
        out[v] = out[v] + phi[v] * q
    out[m] = out[m] + phi[0] + qr
    return out, pb


def pressure_back(g, pb, cell):
    part = 0.4 * pb
    return [
        g[0] + part * cell(KE),
        g[1] - part * cell(V1),
        g[2] - part * cell(V2),
        g[3] - part * cell(V3),
        g[4] + part,
    ]


def kernel(
    base_offset,
    choices,
    step_ref,
    flow_ref,
    adjoint_ref,
    later_ref,
    objective_ref,
    volume_ref,
    maps_ref,
    out_ref,
    state,
    lam,
    cells,
    xcf,
    tcf,
    lcf,
    wcf,
    wcell,
    wu,
    grad,
    gradp,
    upd,
    edge_send,
    edge_recv,
    row_send,
    row_recv,
    flow_send,
    flow_recv,
    panel_send,
    panel_recv,
    ghost,
    send_sem,
    recv_sem,
    panel_send_sem,
    panel_recv_sem,
):
    sectors = lax.axis_size("sector")
    blocks = lax.axis_size("block")
    half = blocks // 2
    sec = lax.axis_index("sector")
    blk = lax.axis_index("block")
    right = lax.rem(sec + 1, sectors)
    left = lax.rem(sec + sectors - 1, sectors)
    slots = min(choices + 1, sectors)
    has_up = jnp.logical_and(blk != half - 1, blk != blocks - 1)
    has_down = jnp.logical_and(blk != 0, blk != half)
    on_rotor = blk == half - 1
    on_stator = blk == half
    on_face = jnp.logical_or(on_rotor, on_stator)
    turn = jnp.where(on_rotor, 1, -1)
    across = blk + turn

    def partner(slot):
        return lax.rem(sec + turn * (base_offset + slot) + 2 * sectors, sectors)

    barrier = pltpu.get_barrier_semaphore()

    def greet(sector, block):
        pl.semaphore_signal(
            barrier, inc=1, device_id={"sector": sector, "block": block}, device_id_type=MESH
        )

    greet(left, blk)
    greet(right, blk)

    @pl.when(has_up)
    def _():
        greet(sec, blk + 1)

    @pl.when(has_down)
    def _():
        greet(sec, blk - 1)

    @pl.when(on_face)
    def _():
        for slot in range(slots):
            greet(partner(slot), across)

    expected = (
        2
        + jnp.where(has_up, 1, 0)
        + jnp.where(has_down, 1, 0)
        + jnp.where(on_face, slots, 0)
    )

    def remote(src, dst, ssem, rsem, sector, block):
        return pltpu.make_async_remote_copy(
            src_ref=src,
            dst_ref=dst,
            send_sem=ssem,
            recv_sem=rsem,
            device_id={"sector": sector, "block": block},
            device_id_type=MESH,
        )

    def edge_copies(r):
        return (
            remote(edge_send.at[r], edge_recv.at[r, 1], send_sem.at[r, 0], recv_sem.at[r, 1], left, blk),
            remote(edge_send.at[r], edge_recv.at[r, 0], send_sem.at[r, 1], recv_sem.at[r, 0], right, blk),
        )

    def row_copies(r, src, dst):
        return (
            remote(src.at[0], dst.at[1], send_sem.at[r, 2], recv_sem.at[r, 3], sec, blk - 1),
            remote(src.at[1], dst.at[0], send_sem.at[r, 3], recv_sem.at[r, 2], sec, blk + 1),
        )

    def panel_copies(r):
        return [
            remote(
                panel_send.at[r],
                panel_recv.at[r, slot],
                panel_send_sem.at[r, slot],
                panel_recv_sem.at[r, slot],
                partner(slot),
                across,
            )
            for slot in range(slots)
        ]

    lane = lax.broadcasted_iota(jnp.int32, (8, 128), 1)
    place = lane & 15
    group = lane >> 4
    low_place = place < 8
    is_edge = jnp.logical_or(lane < 3, lane >= 125)

    def pack_edges(src, r):
        for v in range(5):
            packed = jnp.zeros((8, 128), jnp.float32)
            for g in range(8):
                tile = src[v, g // 2, (g % 2) * 8 : (g % 2) * 8 + 8, :]
                packed = jnp.where(group == g, pltpu.roll(tile, (16 * g + 8) % 128, 1), packed)
            edge_send[r, v] = packed

    def pack_rows(src, dst, width):
        for v in range(5):
            for l in range(4):
                rows = pl.ds(width * l, width)
                dst[0, v, rows, :] = src[v, l, 0:width, :]
                dst[1, v, rows, :] = src[v, l, 16 - width : 16, :]

    def unpack_edges(r, dst):
        for v in range(5):
            own = edge_send[r, v]
            dst[v, 4, 0:8, :] = jnp.where(low_place, own, edge_recv[r, 1, v])
            dst[v, 4, 8:16, :] = jnp.where(low_place, edge_recv[r, 0, v], own)

    for v in range(5):
        for l in range(4):
            state[v, l, 0:16, :] = flow_ref[v, l]
            lam[v, l, 0:16, :] = adjoint_ref[v, l]
            lam[v, l, 16:24, :] = jnp.zeros((8, 128), jnp.float32)
    pack_edges(state, 0)
    pack_rows(state, flow_send, 4)

    @pl.when(on_rotor)
    def _():
        for v in range(5):
            for l in range(4):
                panel_send[0, v, 2 * l : 2 * l + 2, :] = state[v, l, 14:16, :]

    @pl.when(on_stator)
    def _():
        for v in range(5):
            for l in range(4):
                panel_send[0, v, 2 * l : 2 * l + 2, :] = state[v, l, 0:2, :]

    pl.semaphore_wait(barrier, expected)

    @pl.when(on_face)
    def _():
        for copy in panel_copies(0):
            copy.start()

    for copy in edge_copies(0):
        copy.start()
    flow_down, flow_up = row_copies(0, flow_send, flow_recv)

    @pl.when(has_down)
    def _():
        flow_down.start()

    @pl.when(has_up)
    def _():
        flow_up.start()

    phase = lax.rem(step_ref[0], PHASES)
    choice = step_ref[0] // PHASES - base_offset

    def pick(r, wanted):
        out = panel_recv[r, 0]
        for slot in range(1, slots):
            out = jnp.where(wanted == slot, panel_recv[r, slot], out)
        return out.reshape(40, 128)

    def pick_pair(r):
        near = pick(r, choice)
        far = pick(r, choice + 1 if choices < sectors else lax.rem(choice + 1, sectors))
        return near, far

    for copy in edge_copies(0):
        copy.wait()
    unpack_edges(0, state)
    for v in range(5):
        state[v, 4, 16:24, :] = state[v, 4, 0:8, :]

    @pl.when(has_down)
    def _():
        flow_down.wait_send()
        remote(
            flow_send.at[1], flow_recv.at[0], send_sem.at[0, 3], recv_sem.at[0, 2], sec, blk - 1
        ).wait_recv()
        for v in range(5):
            for l in range(4):
                state[v, l, 20:24, :] = flow_recv[0, v, 4 * l : 4 * l + 4, :]

    @pl.when(has_up)
    def _():
        flow_up.wait_send()
        remote(
            flow_send.at[0], flow_recv.at[1], send_sem.at[0, 2], recv_sem.at[0, 3], sec, blk + 1
        ).wait_recv()
        for v in range(5):
            for l in range(4):
                state[v, l, 16:20, :] = flow_recv[1, v, 4 * l : 4 * l + 4, :]

    @pl.when(jnp.logical_not(has_down))
    def _():
        for v in range(5):
            for l in range(4):
                state[v, l, 20:24, :] = jnp.broadcast_to(state[v, l, 0:1, :], (4, 128))

    @pl.when(jnp.logical_not(has_up))
    def _():
        for v in range(5):
            for l in range(4):
                state[v, l, 16:20, :] = jnp.broadcast_to(state[v, l, 15:16, :], (4, 128))

    @pl.when(on_face)
    def _():
        for copy in panel_copies(0):
            copy.wait()
        near, far = pick_pair(0)
        first = jnp.where(on_rotor, 2, 0)
        dims = (((1,), (1,)), ((), ()))
        made = lax.dot_general(
            near, maps_ref[phase, first], dims, precision=HIGHEST, preferred_element_type=jnp.float32
        ) + lax.dot_general(
            far, maps_ref[phase, first + 1], dims, precision=HIGHEST, preferred_element_type=jnp.float32
        )
        ghost[...] = made.reshape(5, 8, 128)

    @pl.when(on_rotor)
    def _():
        for v in range(5):
            for l in range(4):
                state[v, l, 16:18, :] = ghost[v, 2 * l : 2 * l + 2, :]

    @pl.when(on_stator)
    def _():
        for v in range(5):
            for l in range(4):
                state[v, l, 22:24, :] = ghost[v, 2 * l : 2 * l + 2, :]

    x_up, x_down = shifts(0, 24)
    t_up, t_down = shifts(1, 128)
    w_up, w_down = shifts(0, 8)

    def set_cells(l, _):
        u = [state[v, l] for v in range(5)]
        rinv, vel, ke, p, c, rp, rr = cell_terms(u)
        for k, a in enumerate([rinv, vel[0], vel[1], vel[2], u[4] + p, rp, rr, ke]):
            cells[l, k] = a
        ut = [a[0:16] for a in u]
        cf, t_radius = direction_coefs(ut, p[0:16], c[0:16], vel[1][0:16], t_up, t_down)
        for k, a in enumerate(cf):
            tcf[l, k] = a
        return 0

    lax.fori_loop(0, 5, set_cells, 0)

    def set_x(l, _):
        u = [state[v, l] for v in range(5)]
        p = cells[l, ENTH] - u[4]
        vx = cells[l, V1]
        c = -2.0 * cells[l, RR] * u[0]
        cf, _ = direction_coefs(u, p, c, vx, x_up, x_down)
        for k, a in enumerate(cf):
            xcf[l, k] = a
        vol = volume_ref[l]
        rad = 3.0 * c[0:16]
        for k in (V1, V2, V3):
            q = cells[l, k, 0:16]
            rad = rad + jnp.sqrt(q * q + 0.01)
        factor = 0.6 / (rad + 0.45 * vol)
        upd[l, 0] = factor
        upd[l, 1] = 0.75 * factor * vol
        for v in range(5):
            source = objective_ref[v, l] + vol * (
                2.0 * later_ref[0, v, l] - 0.5 * later_ref[1, v, l]
            ) * 0.5
            upd[l, 2 + v] = factor * source
        return 0

    lax.fori_loop(0, 4, set_x, 0)

    def at_rows(half_at):
        return pl.ds(pl.multiple_of(half_at * 8, 8), 8)

    def set_l(half_at, _):
        rows = at_rows(half_at)
        u = [[state[v, l, rows, :] for v in range(5)] for l in range(4)]
        p = [cells[l, ENTH, rows, :] - u[l][4] for l in range(4)]
        q = [cells[l, V3, rows, :] for l in range(4)]
        sq = [jnp.sqrt(a * a + 0.01) for a in q]
        rad = [sq[l] - 2.0 * cells[l, RR, rows, :] * u[l][0] for l in range(4)]

        def clamp(l):
            return min(max(l, 0), 3)

        sens = [sensor_terms(p[clamp(j - 1)], p[clamp(j)], p[clamp(j + 1)]) for j in range(-1, 5)]
        zero = jnp.zeros((8, 128), jnp.float32)
        d1 = {f: [zero] * 5 for f in (-2, -1, 3, 4)}
        for f in range(3):
            d1[f] = [u[f + 1][v] - u[f][v] for v in range(5)]
        for f in range(-1, 4):
            d3 = [d1[f + 1][v] - 2.0 * d1[f][v] + d1[f - 1][v] for v in range(5)]
            faces = face_terms(
                sens[f + 1][0], sens[f + 2][0], rad[clamp(f)], rad[clamp(f + 1)], d1[f], d3
            )
            for k, a in enumerate(faces):
                lcf[f + 1, k, rows, :] = a
        for j in range(6):
            lcf[j, N1, rows, :] = sens[j][1]
            lcf[j, N0, rows, :] = sens[j][2]
        for l in range(4):
            lcf[l, RQ, rows, :] = q[l] / sq[l]
        return 0

    lax.fori_loop(0, 2, set_l, 0)

    at_end = jnp.logical_not(jnp.logical_and(has_up, has_down))
    low_end = jnp.logical_not(has_down)
    high_end = jnp.logical_not(has_up)

    @pl.when(low_end)
    def _():
        def window(ref, l, k):
            return jnp.concatenate([ref[l, k, 20:24, :], ref[l, k, 0:4, :]], axis=0)

        for l in range(4):
            for k in range(NDIR):
                wcf[l, k] = window(xcf, l, k)
            for k in range(NCELL):
                wcell[l, k] = window(cells, l, k)
            for v in range(1, 4):
                wu[l, v] = window(state, v, l)

    @pl.when(high_end)
    def _():
        for l in range(4):
            for k in range(NDIR):
                wcf[l, k] = xcf[l, k, 12:20, :]
            for k in range(NCELL):
                wcell[l, k] = cells[l, k, 12:20, :]
            for v in range(1, 4):
                wu[l, v] = state[v, l, 12:20, :]


    def iterate(k, _):
        r = k + 1
        pack_edges(lam, r)
        pack_rows(lam, row_send.at[r], 2)
        for copy in edge_copies(r):
            copy.start()
        to_down, to_up = row_copies(r, row_send.at[r], row_recv.at[r])

        @pl.when(has_down)
        def _():
            to_down.start()

        @pl.when(has_up)
        def _():
            to_up.start()

        @pl.when(at_end)
        def _():
            def end_rows(l, _):
                low = [jnp.concatenate([jnp.zeros((4, 128), jnp.float32), lam[v, l, 0:4, :]], axis=0) for v in range(5)]
                high = [jnp.concatenate([lam[v, l, 12:16, :], jnp.zeros((4, 128), jnp.float32)], axis=0) for v in range(5)]
                lw = [jnp.where(low_end, a, b) for a, b in zip(low, high)]
                g, pb = direction_apply(
                    lw,
                    lambda n: wcf[l, n],
                    lambda n: wcell[l, n],
                    lambda v: wu[l, v],
                    1,
                    w_up,
                    w_down,
                )
                g = pressure_back(g, pb, lambda n: wcell[l, n])
                for v in range(5):
                    wu[l, 4 + v] = g[v]
                return 0

            lax.fori_loop(0, 4, end_rows, 0)

        @pl.when(low_end)
        def _():
            for v in range(5):
                for l in range(4):
                    panel_send[r, v, 2 * l : 2 * l + 2, :] = wu[l, 4 + v, 2:4, :]

        @pl.when(high_end)
        def _():
            for v in range(5):
                for l in range(4):
                    panel_send[r, v, 2 * l : 2 * l + 2, :] = wu[l, 4 + v, 4:6, :]

        @pl.when(on_face)
        def _():
            for copy in panel_copies(r):
                copy.start()

        def apply_t(l):
            return direction_apply(
                [lam[v, l, 0:16, :] for v in range(5)],
                lambda n: tcf[l, n],
                lambda n: cells[l, n, 0:16, :],
                lambda v: state[v, l, 0:16, :],
                2,
                t_up,
                t_down,
            )

        lane16 = lax.broadcasted_iota(jnp.int32, (16, 128), 1)
        edge16 = jnp.logical_or(lane16 < 3, lane16 >= 125)

        def along_t(l, _):
            g, pb = apply_t(l)
            for v in range(5):
                grad[v, l] = jnp.where(edge16, 0.0, g[v])
            gradp[l] = jnp.where(edge16, 0.0, pb)
            return 0

        lax.fori_loop(0, 4, along_t, 0)

        def along_l(half_at, _):
            rows = at_rows(half_at)
            la = [[lam[v, l, rows, :] for v in range(5)] for l in range(4)]
            w = [[-a for a in la[0]]]
            for f in range(3):
                w.append([la[f][v] - la[f + 1][v] for v in range(5)])
            w.append(la[3])
            lb = [dot5(w[f], [lcf[f, DD + v, rows, :] for v in range(5)]) for f in range(5)]
            eb = [dot5(w[f], [lcf[f, EE + v, rows, :] for v in range(5)]) for f in range(5)]
            nub = [eb[0]] + [eb[f] + eb[f + 1] for f in range(4)] + [eb[4]]
            t1 = [nub[j] * lcf[j, N1, rows, :] for j in range(6)]
            t0 = [nub[j] * lcf[j, N0, rows, :] for j in range(6)]
            far = [[lcf[f, LE4, rows, :] * w[f][v] for v in range(5)] for f in range(5)]
            z = []
            for f in range(1, 4):
                z.append(
                    [
                        far[f - 1][v] + far[f + 1][v] - 2.0 * far[f][v] - lcf[f, LE2, rows, :] * w[f][v]
                        for v in range(5)
                    ]
                )
            for l in range(4):
                rb = lb[l] + lb[l + 1]
                phi = [0.5 * (w[l][v] + w[l + 1][v]) for v in range(5)]
                pb = t1[l] + t1[l + 2] + t0[l + 1]
                if l == 0:
                    rb = rb + lb[0]
                    phi = [phi[v] + 0.5 * w[0][v] for v in range(5)]
                    pb = pb + t1[1] + t0[0] + t1[0]
                if l == 3:
                    rb = rb + lb[4]
                    phi = [phi[v] + 0.5 * w[4][v] for v in range(5)]
                    pb = pb + t1[4] + t0[5] + t1[5]
                q = cells[l, V3, rows, :]
                qb = (
                    rb * lcf[l, RQ, rows, :]
                    + phi[1] * state[1, l, rows, :]
                    + phi[2] * state[2, l, rows, :]
                    + phi[3] * state[3, l, rows, :]
                    + phi[4] * cells[l, ENTH, rows, :]
                )
                pb = pb + rb * cells[l, RP, rows, :] + phi[4] * q + phi[3]
                if l == 0:
                    g = [-a for a in z[0]]
                elif l == 3:
                    g = list(z[2])
                else:
                    g = [a - b for a, b in zip(z[l - 1], z[l])]
                qr = qb * cells[l, RINV, rows, :]
                g[0] = g[0] + rb * cells[l, RR, rows, :] - qr * q
                for v in range(1, 5):
                    g[v] = g[v] + phi[v] * q
                g[3] = g[3] + phi[0] + qr
                for v in range(5):
                    grad[v, l, rows, :] += g[v]
                gradp[l, rows, :] += pb
            return 0

        lax.fori_loop(0, 2, along_l, 0)

        for copy in edge_copies(r):
            copy.wait()
        unpack_edges(r, lam)
        g, pb = apply_t(4)
        for v in range(5):
            grad[v, 4, 0:8, :] = jnp.where(low_place, g[v][0:8], g[v][8:16])
        gradp[4, 0:8, :] = jnp.where(low_place, pb[0:8], pb[8:16])

        @pl.when(has_down)
        def _():
            to_down.wait_send()
            remote(
                row_send.at[r, 1], row_recv.at[r, 0], send_sem.at[r, 3], recv_sem.at[r, 2], sec, blk - 1
            ).wait_recv()
            for v in range(5):
                for l in range(4):
                    lam[v, l, 22:24, :] = row_recv[r, 0, v, 2 * l : 2 * l + 2, :]

        @pl.when(has_up)
        def _():
            to_up.wait_send()
            remote(
                row_send.at[r, 0], row_recv.at[r, 1], send_sem.at[r, 2], recv_sem.at[r, 3], sec, blk + 1
            ).wait_recv()
            for v in range(5):
                for l in range(4):
                    lam[v, l, 16:18, :] = row_recv[r, 1, v, 2 * l : 2 * l + 2, :]

        def along_x(l, _):
            la = [lam[v, l] for v in range(5)]
            g, pb = direction_apply(
                la,
                lambda n: xcf[l, n],
                lambda n: cells[l, n],
                lambda v: state[v, l],
                1,
                x_up,
                x_down,
            )

            def spread(tile):
                parts = []
                for half_at in range(2):
                    by = lax.rem(248 - 32 * l - 16 * half_at, 128)
                    parts.append(jnp.where(is_edge, pltpu.roll(tile, by, 1), 0.0))
                return jnp.concatenate(parts, axis=0)

            g = [g[v][0:16] + grad[v, l] + spread(grad[v, 4, 0:8, :]) for v in range(5)]
            pb = pb[0:16] + gradp[l] + spread(gradp[4, 0:8, :])
            g = pressure_back(g, pb, lambda n: cells[l, n, 0:16, :])
            for v in range(5):
                old = la[v][0:16]
                lam[v, l, 0:16, :] = old - (upd[l, 1] * old + upd[l, 0] * g[v] - upd[l, 2 + v])
            return 0

        lax.fori_loop(0, 4, along_x, 0)

        @pl.when(on_face)
        def _():
            for copy in panel_copies(r):
                copy.wait()
            near, far = pick_pair(r)
            first = jnp.where(on_rotor, 0, 2)
            made = jnp.dot(
                near, maps_ref[phase, first], precision=HIGHEST, preferred_element_type=jnp.float32
            ) + jnp.dot(
                far, maps_ref[phase, first + 1], precision=HIGHEST, preferred_element_type=jnp.float32
            )
            ghost[...] = made.reshape(5, 8, 128)

        @pl.when(jnp.logical_and(at_end, jnp.logical_not(on_face)))
        def _():
            parity = lax.broadcasted_iota(jnp.int32, (8, 128), 0) & 1
            even = parity == 0
            keep = parity == jnp.where(low_end, 0, 1)
            for v in range(5):
                a = panel_send[r, v]
                both = a + jnp.where(even, pltpu.roll(a, 7, 0), pltpu.roll(a, 1, 0))
                ghost[v] = jnp.where(keep, both, 0.0)

        @pl.when(low_end)
        def _():
            for v in range(5):
                for l in range(4):
                    lam[v, l, 0:2, :] -= upd[l, 0, 0:2, :] * ghost[v, 2 * l : 2 * l + 2, :]

        @pl.when(high_end)
        def _():
            for v in range(5):
                for l in range(4):
                    lam[v, l, 14:16, :] -= upd[l, 0, 14:16, :] * ghost[v, 2 * l : 2 * l + 2, :]

        return 0

    lax.fori_loop(0, ITERS, iterate, 0)
    for v in range(5):
        for l in range(4):
            out_ref[v, l] = lam[v, l, 0:16, :]


def run(base_offset, choices, index, sectors, *args):
    slots = min(choices + 1, sectors)
    f32 = jnp.float32
    vmem = pl.BlockSpec(memory_space=pltpu.VMEM)
    return pl.pallas_call(
        functools.partial(kernel, base_offset, choices),
        out_shape=jax.ShapeDtypeStruct(args[1].shape, f32),
        in_specs=[pl.BlockSpec(memory_space=pltpu.SMEM)] + [vmem] * 6,
        out_specs=vmem,
        scratch_shapes=[
            pltpu.VMEM((5, 5, 24, 128), f32),
            pltpu.VMEM((5, 5, 24, 128), f32),
            pltpu.VMEM((5, NCELL, 24, 128), f32),
            pltpu.VMEM((4, NDIR, 24, 128), f32),
            pltpu.VMEM((5, NDIR, 16, 128), f32),
            pltpu.VMEM((6, NDIR, 16, 128), f32),
            pltpu.VMEM((4, NDIR, 8, 128), f32),
            pltpu.VMEM((4, NCELL, 8, 128), f32),
            pltpu.VMEM((4, 9, 8, 128), f32),
            pltpu.VMEM((5, 5, 16, 128), f32),
            pltpu.VMEM((5, 16, 128), f32),
            pltpu.VMEM((4, 7, 16, 128), f32),
            pltpu.VMEM((ROUNDS, 5, 8, 128), f32),
            pltpu.VMEM((ROUNDS, 2, 5, 8, 128), f32),
            pltpu.VMEM((ROUNDS, 2, 5, 8, 128), f32),
            pltpu.VMEM((ROUNDS, 2, 5, 8, 128), f32),
            pltpu.VMEM((2, 5, 16, 128), f32),
            pltpu.VMEM((2, 5, 16, 128), f32),
            pltpu.VMEM((ROUNDS, 5, 8, 128), f32),
            pltpu.VMEM((ROUNDS, slots, 5, 8, 128), f32),
            pltpu.VMEM((5, 8, 128), f32),
            pltpu.SemaphoreType.DMA((ROUNDS, 4)),
            pltpu.SemaphoreType.DMA((ROUNDS, 4)),
            pltpu.SemaphoreType.DMA((ROUNDS, slots)),
            pltpu.SemaphoreType.DMA((ROUNDS, slots)),
        ],
        compiler_params=pltpu.CompilerParams(collective_id=index, has_side_effects=True),
        name="adjoint_sweeps",
    )(*args)


def shards(flow, adjoint, adjoint_later, objective_grad, volume, panel_maps, rotor_step):
    sectors = lax.axis_size("sector")
    args = (rotor_step, flow, adjoint, adjoint_later, objective_grad, volume, panel_maps)
    choices = min(CHOICES, sectors)
    count = sectors // choices
    branches = [
        functools.partial(run, i * choices, choices, i, sectors) for i in range(count)
    ]
    if count == 1:
        return branches[0](*args)
    offset = rotor_step[0] // PHASES
    return lax.switch(offset // choices, branches, *args)


def solution(mesh):
    placed = (
        P(None, None, "block", "sector"),
        P(None, None, "block", "sector"),
        P(None, None, None, "block", "sector"),
        P(None, None, "block", "sector"),
        P(None, "block", "sector"),
        P(),
        P(),
    )
    return jax.shard_map(
        shards,
        mesh=mesh,
        in_specs=placed,
        out_specs=P(None, None, "block", "sector"),
        check_vma=False,
    )
```

time: 740 us -> 74.8 us (0.10)
  the two profiles are of different devices: /device:TPU:64 before, /device:TPU:129 now
where the time goes in v1:
time: 74.8 us; the launch traced here: 74.6 us
  Pallas kernels  72.4 us (97%)
  local copies, waits for them, and re-layouts  1.59 us (2%)
    pallas_call x1, Pallas kernels, run(): pl.pallas_call(functools.partial(kernel, base_offset, choices), out_shape...  72.4 us
    unnamed x1, local copies, waits for them, and re-layouts  1.59 us

profile of v1, /device:TPU:129, one launch (start us, length us, event | category | flops | bytes accessed | tf_op | source)
XLA Modules:
  0.0 74.6 jit_solution(16972135792912079895)
XLA Ops:
  0.7 72.4 %adjoint_sweeps.1 = f32[5,4,16,128]{3,2,1,0:T(8,128)} custom-call(s32[1]{0:T(128)S(6)} %copy.9.step_ref, f32[5,4,16,128]{3,2,1,0:T(8,128)} %flow_ref.1, f32[5,4,16,128]{3,2,1,0:T(8,128)} %adjoint_ref.1, f32[2,5,4,16,128]{4,3,2,1,0:T(8,128)} %later_ref.1, f32[5,4,16,128]{3,2,1,0:T(8,128)} %objective_ref.1, f32[4,16,128]{2,1,0:T(8,128)} %volume_ref.1, ...), custom_call_target="tpu_custom_call" | custom-call | tf_op jit(solution)/shard_map/adjoint_sweeps/pallas_call | solution.py:724
  73.0 1.6 %copy.10 = f32[5,4,16,128]{3,2,1,0:T(8,128)} copy(f32[5,4,16,128]{3,2,1,0:T(8,128)} %adjoint_sweeps.1) | data formatting | bytes 327680
